TPU v7x, 128 devices: a whole 4x4x4 slice. The times are simulated.
128 devices in a mesh: dp: 32 (over x, y, core), pair: 4 (over z).
Axes of the slice: x: 4, y: 4, z: 4, core: 2. Of those that a mesh axis runs over, the one named last changes fastest.
Arguments:
- local_grads: bfloat16 [128, 1536, 4096], P(('dp', 'pair')), may hold values from -512 to 512, as said below
- error_feedback: bfloat16 [128, 1536, 4096], P(('dp', 'pair')), may hold values from -6 to 6
- q_start: float32 [4096, 32], replicated, may hold values from -0.09375 to 0.09375
Outputs:
- left_out: float32 [1536, 32], P(('dp', 'pair'))
- right_out: float32 [4096, 32], P(('dp', 'pair'))
Inputs may be any that keep to these rules, and one draw needn't show every extreme that they name: `local_grads`: each replica's own gradient.
All inputs are finite; a program needn't handle non-finite values.
Results may differ from a plain program's by a relative error of at most 0.0003.
Values sent between devices are 32-bit elements; how exact they have to be, the bound alone decides.
A program may use at most 128 MiB of HBM per device.

v0:
```python
import jax
import jax.numpy as jnp
from jax import lax
from jax.sharding import PartitionSpec as P

ITERS = 2


def gram_matrix(factor):
    return jnp.dot(factor.T, factor, precision=lax.Precision.HIGHEST)


def orthonormal(factor, gram_total):
    lower_factor = jnp.linalg.cholesky(gram_total)
    return jax.scipy.linalg.solve_triangular(lower_factor, factor.T, lower=True).T


def times_factor(merged_block, factor):
    return jnp.dot(merged_block, factor, precision=lax.Precision.HIGHEST)


def transposed_times(merged_block, factor):
    return lax.dot_general(
        merged_block, factor, (((0,), (0,)), ((), ())), precision=lax.Precision.HIGHEST
    )


def shards(local_grads, error_feedback, q_start):
    group_size = lax.axis_size(("dp", "pair"))
    position = lax.axis_index(("dp", "pair"))
    merged = local_grads[0].astype(jnp.float32) + error_feedback[0].astype(jnp.float32)
    depth_rows = merged.shape[0]
    width_cols = merged.shape[1]
    left_share = depth_rows // group_size
    right_share = width_cols // group_size
    basis_now = q_start
    left_factor = None
    right_factor = None
    for iteration in range(ITERS):
        left_term = times_factor(merged, basis_now)
        left_factor = lax.psum(left_term, ("dp", "pair")) / group_size
        left_basis = orthonormal(left_factor, gram_matrix(left_factor))
        right_term = transposed_times(merged, left_basis)
        right_factor = lax.psum(right_term, ("dp", "pair")) / group_size
        if iteration + 1 < ITERS:
            basis_now = orthonormal(right_factor, gram_matrix(right_factor))
    left_out = lax.dynamic_slice_in_dim(left_factor, position * left_share, left_share, 0)
    right_out = lax.dynamic_slice_in_dim(right_factor, position * right_share, right_share, 0)
    return (left_out, right_out)


def solution(mesh):
    return jax.shard_map(
        shards,
        mesh=mesh,
        in_specs=(P(("dp", "pair"), None, None), P(("dp", "pair"), None, None), P()),
        out_specs=(P(("dp", "pair"), None), P(("dp", "pair"), None)),
        check_vma=False,
    )
```

profile of v0, /device:TPU:1, one launch (start us, length us, event | category | flops | bytes accessed | tf_op | source)
XLA Modules:
  0.0 722.1 jit_solution(17965734013922250561)
XLA Ops:
  7.2 1.0 copy-done
  8.2 29.1 %fusion.6 = f32[1536,32]{0,1:T(8,128)} fusion(f32[4096,32]{0,1:T(8,128)S(1)} %copy-done, bf16[1,1536,4096]{2,1,0:T(8,128)(2,1)} %param.7, bf16[1,1536,4096]{2,1,0:T(8,128)(2,1)} %param.6), kind=kOutput, calls=%fused_computation.6 | convolution fusion | flops 2434793472 | bytes 25886720 | tf_op jit(solution)/shard_map/dot_general | solution.py:19
  37.4 146.0 %all-reduce.5.cloned.1.call-done = f32[1536,32]{0,1:T(8,128)} async-done(((f32[1536,32]{0,1:T(8,128)}), f32[1536,32]{0,1:T(8,128)}) %all-reduce.5.cloned.1.call-update) | async-done | bytes 196624 | tf_op jit(solution)/shard_map/psum | solution.py:41
  183.4 1.3 fusion.19
  184.8 2.9 cholesky.59
  187.7 0.6 compare_reduce_fusion.2
  188.4 0.7 fusion.23
  189.0 2.4 custom-call.11
  191.5 1.3 fusion.16
  192.8 22.0 %fusion.4 = f32[4096,32]{0,1:T(8,128)} fusion(f32[32,1536]{1,0:T(8,128)S(1)} %fusion.16, bf16[1,1536,4096]{2,1,0:T(8,128)(2,1)} %param.7, bf16[1,1536,4096]{2,1,0:T(8,128)(2,1)} %param.6), kind=kOutput, calls=%fused_computation.4 | convolution fusion | flops 2434793472 | bytes 25886720 | tf_op jit(solution)/shard_map/dot_general | solution.py:23
  214.8 0.2 all-reduce.9.cloned.1.call-start
  215.0 143.4 %all-reduce.7.cloned.1.call-done = f32[4096,32]{0,1:T(8,128)} async-done(((f32[4096,32]{0,1:T(8,128)}), f32[4096,32]{0,1:T(8,128)}) %all-reduce.7.cloned.1.call-update) | async-done | bytes 524304 | tf_op jit(solution)/shard_map/psum | solution.py:44
  358.4 1.8 fusion.10
  360.3 2.9 cholesky.70
  363.3 0.6 compare_reduce_fusion.1
  363.9 0.7 fusion.24
  364.6 2.4 custom-call.9
  367.0 1.7 fusion.8
  368.7 29.1 %fusion.2 = f32[1536,32]{0,1:T(8,128)} fusion(f32[32,4096]{1,0:T(8,128)S(1)} %fusion.8, bf16[1,1536,4096]{2,1,0:T(8,128)(2,1)} %param.7, bf16[1,1536,4096]{2,1,0:T(8,128)(2,1)} %param.6), kind=kOutput, calls=%fused_computation.2 | convolution fusion | flops 2434793472 | bytes 25886720 | tf_op jit(solution)/shard_map/dot_general | solution.py:19
  397.9 0.3 all-reduce.11.cloned.1.call-start
  398.1 140.9 %all-reduce.9.cloned.1.call-done = f32[1536,32]{0,1:T(8,128)} async-done(((f32[1536,32]{0,1:T(8,128)}), f32[1536,32]{0,1:T(8,128)}) %all-reduce.9.cloned.1.call-update) | async-done | bytes 196624 | tf_op jit(solution)/shard_map/psum | solution.py:41
  539.0 1.3 fusion.38
  540.4 2.9 cholesky.81
  543.4 0.6 compare_reduce_fusion
  544.0 0.7 fusion.25
  544.7 2.4 custom-call.12
  547.1 1.3 fusion.14
  548.4 22.0 %fusion = f32[4096,32]{0,1:T(8,128)} fusion(f32[32,1536]{1,0:T(8,128)S(1)} %fusion.14, bf16[1,1536,4096]{2,1,0:T(8,128)(2,1)} %param.7, bf16[1,1536,4096]{2,1,0:T(8,128)(2,1)} %param.6), kind=kOutput, calls=%fused_computation | convolution fusion | flops 2434793472 | bytes 25886720 | tf_op jit(solution)/shard_map/dot_general | solution.py:23
  570.6 0.7 copy.9
  571.3 142.9 %all-reduce.11.cloned.1.call-done = f32[4096,32]{0,1:T(8,128)} async-done(((f32[4096,32]{0,1:T(8,128)}), f32[4096,32]{0,1:T(8,128)}) %all-reduce.11.cloned.1.call-update) | async-done | bytes 524304 | tf_op jit(solution)/shard_map/psum | solution.py:44
  714.1 0.8 dynamic-slice_multiply_fusion
  714.9 0.7 copy.10
  (20 shorter events, 0.7 us)
Async XLA Ops:
  7.2 1.0 copy-start
  7.2 176.2 %all-reduce.5.cloned.1.call-start = ((), (), s32[]{:S(2)}) async-start(), calls=%async_computation | async-start | bytes 393216 | tf_op jit(solution)/shard_map/psum | solution.py:41
  37.4 321.1 %all-reduce.7.cloned.1.call-start = ((), (), s32[]{:S(2)}) async-start(), calls=%async_computation.1 | async-start | bytes 1048576 | tf_op jit(solution)/shard_map/psum | solution.py:44
  214.8 324.2 %all-reduce.9.cloned.1.call-start = ((), (), s32[]{:S(2)}) async-start(), calls=%async_computation.2 | async-start | bytes 393216 | tf_op jit(solution)/shard_map/psum | solution.py:41
  397.9 316.3 %all-reduce.11.cloned.1.call-start = ((), (), s32[]{:S(2)}) async-start(), calls=%async_computation.3 | async-start | bytes 1048576 | tf_op jit(solution)/shard_map/psum | solution.py:44
  548.4 22.0 %copy-start.1 = (f32[1536,32]{0,1:T(8,128)S(1)}, f32[1536,32]{0,1:T(8,128)}, u32[]{:S(2)}) copy-start(f32[1536,32]{0,1:T(8,128)} %all-reduce.9.cloned.1.call-done) | copy-start | bytes 589828
Sparse Core Ops, SparseCore 0:
  37.5 145.8 all-reduce.4
  214.9 143.4 all-reduce.6
  398.0 140.9 all-reduce.8
  570.6 143.4 all-reduce.10
where the time goes:
time: 723 us; the launch traced here: 722 us
  waiting for transfers between devices  573 us (79%)
  matrix products  111 us (15%)
  other arithmetic  20.9 us (3%)
  between operations  13.9 us (2%)
    psum x2, waiting for transfers between devices, shards(): left_factor = lax.psum(left_term, ('dp', 'pair')) / group_size  287 us
    psum x2, waiting for transfers between devices, shards(): right_factor = lax.psum(right_term, ('dp', 'pair')) / group_size  286 us
    dot_general x2, matrix products, times_factor(): return jnp.dot(merged_block, factor, precision=lax.Precision.HIGHEST)  58.3 us
    dot_general x2, matrix products, transposed_times(): lax.dot_general(merged_block, factor, (((0,), (0,)), ((), ())), precision...  43.9 us
  transfers between devices with their start and end apart: 4, of which 4 were waited for; matrix products, arithmetic and copies ran while one was open for 0% of the time, Pallas kernels for 0%

commit v1 on v0

v1 whole, which is shorter than its diff:
```python
import jax
import jax.numpy as jnp
from jax import lax
from jax.experimental import pallas as pl
from jax.experimental.pallas import tpu as pltpu
from jax.sharding import PartitionSpec as P

MESH = pl.DeviceIdType.MESH
F32 = jnp.float32
BF16 = jnp.bfloat16
EXACT = lax.Precision.HIGHEST

X, Y, CORES, PAIR = 4, 4, 2, 4
N = X * Y * CORES * PAIR
D, FF, RANK = 1536, 4096, 32
PARTS = 3
GROUPS = RANK // 8
TL = D // 128 * GROUPS
ROWS = 256
COLS = 512
SCALE = 1.0 / N
OUT_L, OUT_R = D // N, FF // N

NT = (((1,), (1,)), ((), ()))


def device(i):
    return (i // PAIR, i % PAIR)


def position():
    return lax.axis_index("dp") * PAIR + lax.axis_index("pair")


def owner_of_left(t):
    return (t * N) // TL


def far_first(k):
    dp, z = lax.axis_index("dp"), lax.axis_index("pair")
    x, y, c = dp // (Y * CORES), (dp // CORES) % Y, dp % CORES

    def step(t):
        return ((3 - t) * (4 - t) // 2) % 4

    x = (x + step(k // 32)) % X
    y = (y + step((k // 8) % 4)) % Y
    z = (z + step((k // 2) % 4)) % PAIR
    c = (c + 1 - k % 2) % CORES
    return ((x * Y + y) * CORES + c, z)


def split(x):
    high = x.astype(BF16)
    rest = x - high.astype(F32)
    mid = rest.astype(BF16)
    low = (rest - mid.astype(F32)).astype(BF16)
    return high, mid, low


def put_parts(ref, columns, x):
    for i, part in enumerate(split(x)):
        ref[i * RANK:(i + 1) * RANK, columns] = part


def add_parts(acc):
    return (acc[2 * RANK:3 * RANK] + acc[RANK:2 * RANK]) + acc[0:RANK]


def lane_group(shape):
    return lax.broadcasted_iota(jnp.int32, shape, 1) // RANK


def regroup(tiles, to):
    group = lane_group((8, 128))
    out = None
    for q, tile in enumerate(tiles):
        moved = pltpu.roll(tile, (RANK * (q - to)) % 128, 1) if q != to else tile
        out = moved if out is None else jnp.where(group == q, moved, out)
    return out


def inverse_factor(parts_ref):
    gram = lax.dot_general(parts_ref[0:PARTS * RANK, :], parts_ref[...], NT, preferred_element_type=F32)
    gram = add_parts(gram)
    gram = (pltpu.roll(gram, 64, 1) + pltpu.roll(gram, 96, 1)) + gram
    lane = lax.broadcasted_iota(jnp.int32, (RANK, 128), 1)
    row = lax.broadcasted_iota(jnp.int32, (RANK, 128), 0)
    both = jnp.where(lane < RANK, gram, jnp.where(lane == row + RANK, 1.0, 0.0))
    for k in range(RANK - 1):
        pivot_row = both[k:k + 1, :]
        scaled = pivot_row / both[k:k + 1, k:k + 1]
        factor = jnp.where(row > k, jnp.broadcast_to(both[:, k:k + 1], (RANK, 128)), 0.0)
        both = both - factor * scaled
    pivots = jnp.sum(jnp.where(lane == row, both, 0.0), axis=1, keepdims=True)
    return (pltpu.roll(both, 96, 1) / jnp.sqrt(pivots))[:, 0:RANK]


def total(ref):
    sums = [jnp.sum(ref[i * 16:(i + 1) * 16], axis=0) for i in range(N // 16)]
    while len(sums) > 1:
        sums = [a + b for a, b in zip(sums[::2], sums[1::2])]
    return sums[0] * SCALE


def wait_tiles(ref, count, sem):
    pltpu.make_async_copy(ref.at[pl.ds(0, count)], ref.at[pl.ds(0, count)], sem).wait()


def kernel(
    grads, errors, start, left_out, right_out,
    g, e, q, b_parts, l_parts, l_send, l_recv, l_all, r_send, r_recv, r_all, tile, left, load_sem, send_sem, recv_sem,
):
    me = position()
    my_left = (me * TL + N - 1) // N
    owns_left = jnp.logical_and(my_left < TL, owner_of_left(my_left) == me)
    chunks = D // ROWS
    first_chunk = (me * chunks) // N + chunks // 2

    def load(i):
        rows = pl.ds(pl.multiple_of(((first_chunk + i) % chunks) * ROWS, ROWS), ROWS)
        return (
            pltpu.make_async_copy(grads.at[0, rows, :], g.at[rows, :], load_sem.at[i]),
            pltpu.make_async_copy(errors.at[0, rows, :], e.at[rows, :], load_sem.at[chunks + i]),
        )

    q_copy = pltpu.make_async_copy(start, q, load_sem.at[2 * chunks])
    q_copy.start()
    for i in range(chunks):
        for copy in load(i):
            copy.start()

    barrier = pltpu.get_barrier_semaphore()

    def greet(k, carry):
        pl.semaphore_signal(barrier, inc=1, device_id=device((me + k) % N), device_id_type=MESH)
        return carry

    lax.fori_loop(1, N, greet, 0)

    b_parts[PARTS * RANK:, :] = jnp.zeros((128 - PARTS * RANK, FF), BF16)
    l_parts[PARTS * RANK:, :] = jnp.zeros((128 - PARTS * RANK, D), BF16)
    left[:, D:] = jnp.zeros((RANK, 128), F32)
    q_copy.wait()

    def turn(j, carry):
        rows = pl.ds(pl.multiple_of(j * 128, 128), 128)
        put_parts(b_parts, rows, q[rows, :].T)
        return carry

    lax.fori_loop(0, FF // 128, turn, 0)

    def to_left_owner(it, t):
        owner = owner_of_left(t)

        @pl.when(owner != me)
        def _():
            pltpu.make_async_remote_copy(
                l_send.at[it, t], l_recv.at[it, me], send_sem.at[2 * it], recv_sem.at[2 * it],
                device_id=device(owner), device_id_type=MESH,
            ).start()

        @pl.when(owner == me)
        def _():
            l_recv[it, me] = l_send[it, t]

    def left_chunk(it, i):
        chunk = (first_chunk + i) % chunks
        rows = pl.ds(pl.multiple_of(chunk * ROWS, ROWS), ROWS)
        parts = b_parts[0:PARTS * RANK, :]
        acc = lax.dot_general(parts, g[rows, :], NT, preferred_element_type=F32)
        acc = acc + lax.dot_general(parts, e[rows, :], NT, preferred_element_type=F32)
        acc = add_parts(acc)
        tiles = ROWS // 128 * GROUPS
        for j in range(tiles):
            lanes = slice(j // GROUPS * 128, j // GROUPS * 128 + 128)
            ranks = slice(j % GROUPS * 8, j % GROUPS * 8 + 8)
            l_send[it, chunk * tiles + j] = acc[ranks, lanes]

        def send(j, carry):
            to_left_owner(it, chunk * tiles + j)
            return carry

        lax.fori_loop(0, tiles, send, 0)

    def right_chunk(it, i):
        steps = FF // COLS
        chunk = ((me * steps) // N + steps // 2 + i) % steps
        columns = pl.ds(pl.multiple_of(chunk * COLS, COLS), COLS)
        parts = l_parts[0:PARTS * RANK, :]
        acc = jnp.dot(parts, g[:, columns], preferred_element_type=F32)
        acc = acc + jnp.dot(parts, e[:, columns], preferred_element_type=F32)
        acc = add_parts(acc)
        owners = COLS // OUT_R
        for j in range(COLS // 128):
            tiles = [acc[r * 8:r * 8 + 8, j * 128:j * 128 + 128] for r in range(GROUPS)]
            for r in range(128 // OUT_R):
                r_send[it, chunk * owners + j * (128 // OUT_R) + r] = regroup(tiles, r)

        def send(j, carry):
            owner = chunk * owners + j

            @pl.when(owner != me)
            def _():
                pltpu.make_async_remote_copy(
                    r_send.at[it, owner], r_recv.at[it, me], send_sem.at[2 * it + 1], recv_sem.at[2 * it + 1],
                    device_id=device(owner), device_id_type=MESH,
                ).start()

            @pl.when(owner == me)
            def _():
                r_recv[it, me] = r_send[it, owner]

            return carry

        lax.fori_loop(0, owners, send, 0)

    def send_left_sums(it):
        @pl.when(owns_left)
        def _():
            wait_tiles(l_recv.at[it], N - 1, recv_sem.at[2 * it])
            tile[it] = total(l_recv.at[it])

            def send(k, carry):
                pltpu.make_async_remote_copy(
                    tile.at[it], l_all.at[it, my_left], send_sem.at[4 + it], recv_sem.at[4 + it],
                    device_id=far_first(k), device_id_type=MESH,
                ).start()
                return carry

            lax.fori_loop(0, N - 1, send, 0)
            l_all[it, my_left] = tile[it]
            wait_tiles(l_all.at[it], TL - 1, recv_sem.at[4 + it])

        @pl.when(jnp.logical_not(owns_left))
        def _():
            wait_tiles(l_all.at[it], TL, recv_sem.at[4 + it])

    def right_sum(it, inverse):
        wait_tiles(r_recv.at[it], N - 1, recv_sem.at[2 * it + 1])
        summed = total(r_recv.at[it])
        ranks = [pltpu.roll(summed, (128 - RANK * r) % 128, 1) if r else summed for r in range(GROUPS)]
        return jnp.dot(inverse, jnp.concatenate(ranks, axis=0), precision=EXACT, preferred_element_type=F32)

    for i in range(chunks):
        for copy in load(i):
            copy.wait()
        if i == 0:
            pl.semaphore_wait(barrier, N - 1)
        left_chunk(0, i)
    send_left_sums(0)
    for j in range(D // 128):
        block = jnp.concatenate([l_all[0, j * GROUPS + r] for r in range(GROUPS)], axis=0)
        put_parts(l_parts, slice(j * 128, j * 128 + 128), block)
    lax.fori_loop(0, FF // COLS, lambda i, carry: (right_chunk(0, i), carry)[1], 0)
    inverse = inverse_factor(l_parts)
    mine = right_sum(0, inverse)
    packed = mine[0:8]
    group = lane_group((8, 128))
    for r in range(1, GROUPS):
        packed = jnp.where(group == r, pltpu.roll(mine[r * 8:r * 8 + 8], RANK * r, 1), packed)
    tile[2] = packed

    def send_right(k, carry):
        pltpu.make_async_remote_copy(
            tile.at[2], r_all.at[me], send_sem.at[6], recv_sem.at[6],
            device_id=far_first(k), device_id_type=MESH,
        ).start()
        return carry

    lax.fori_loop(0, N - 1, send_right, 0)
    r_all[me] = tile[2]
    wait_tiles(r_all, N - 1, recv_sem.at[6])

    def gather_right(j, carry):
        tiles = [r_all[j * 4 + r] for r in range(4)]
        block = jnp.concatenate([regroup(tiles, r) for r in range(GROUPS)], axis=0)
        put_parts(b_parts, pl.ds(pl.multiple_of(j * 128, 128), 128), block)
        return carry

    lax.fori_loop(0, FF // 128, gather_right, 0)

    lax.fori_loop(0, chunks, lambda i, carry: (left_chunk(1, i), carry)[1], 0)
    inverse = inverse_factor(b_parts)
    send_left_sums(1)
    for j in range(D // 512):
        block = jnp.concatenate(
            [
                jnp.concatenate([l_all[1, (j * 4 + i) * GROUPS + r] for r in range(GROUPS)], axis=0)
                for i in range(4)
            ],
            axis=1,
        )
        block = jnp.dot(inverse, block, precision=EXACT, preferred_element_type=F32)
        left[:, j * 512:j * 512 + 512] = block
        put_parts(l_parts, slice(j * 512, j * 512 + 512), block)
    lax.fori_loop(0, FF // COLS, lambda i, carry: (right_chunk(1, i), carry)[1], 0)
    at = (me * OUT_L) // 128
    block = left[:, pl.ds(pl.multiple_of(at * 128, 128), 256)]
    block = pltpu.roll(block, (256 - (me * OUT_L - at * 128)) % 256, 1)[:, 0:128]
    left_out[...] = block.T[0:OUT_L, :]
    inverse = inverse_factor(l_parts)
    mine = right_sum(1, inverse)
    right_out[...] = mine.T[0:OUT_R, :]

    for it in range(2):
        @pl.when(owns_left)
        def _():
            wait_tiles(l_send.at[it], TL - 1, send_sem.at[2 * it])
            wait_tiles(r_send.at[it], N - 1, send_sem.at[4 + it])

        @pl.when(jnp.logical_not(owns_left))
        def _():
            wait_tiles(l_send.at[it], TL, send_sem.at[2 * it])

        wait_tiles(r_send.at[it], N - 1, send_sem.at[2 * it + 1])
    wait_tiles(r_all, N - 1, send_sem.at[6])


def shards(local_grads, error_feedback, q_start):
    anywhere = pl.BlockSpec(memory_space=pl.ANY)
    vmem = pl.BlockSpec(memory_space=pltpu.VMEM)
    return pl.pallas_call(
        kernel,
        out_shape=(
            jax.ShapeDtypeStruct((OUT_L, RANK), F32),
            jax.ShapeDtypeStruct((OUT_R, RANK), F32),
        ),
        in_specs=[anywhere, anywhere, anywhere],
        out_specs=(vmem, vmem),
        scratch_shapes=[
            pltpu.VMEM((D, FF), BF16),
            pltpu.VMEM((D, FF), BF16),
            pltpu.VMEM((FF, RANK), F32),
            pltpu.VMEM((128, FF), BF16),
            pltpu.VMEM((128, D), BF16),
            pltpu.VMEM((2, TL, 8, 128), F32),
            pltpu.VMEM((2, N, 8, 128), F32),
            pltpu.VMEM((2, TL, 8, 128), F32),
            pltpu.VMEM((2, N, 8, 128), F32),
            pltpu.VMEM((2, N, 8, 128), F32),
            pltpu.VMEM((N, 8, 128), F32),
            pltpu.VMEM((3, 8, 128), F32),
            pltpu.VMEM((RANK, D + 128), F32),
            pltpu.SemaphoreType.DMA((2 * (D // ROWS) + 1,)),
            pltpu.SemaphoreType.DMA((7,)),
            pltpu.SemaphoreType.DMA((7,)),
        ],
        compiler_params=pltpu.CompilerParams(
            vmem_limit_bytes=60 << 20, collective_id=0, has_side_effects=True
        ),
    )(local_grads, error_feedback, q_start)


def solution(mesh):
    return jax.shard_map(
        shards,
        mesh=mesh,
        in_specs=(P(("dp", "pair"), None, None), P(("dp", "pair"), None, None), P()),
        out_specs=(P(("dp", "pair"), None), P(("dp", "pair"), None)),
        check_vma=False,
    )
```

time: 723 us -> 124 us (0.17)
  waiting for transfers between devices: 573 us -> 0 us
  Pallas kernels: 0 us -> 118 us
  matrix products: 111 us -> 0 us
  other arithmetic: 20.9 us -> 0 us
  between operations: 13.9 us -> 0.64 us
    psum x4 -> x0, waiting for transfers between devices: 573 us -> none  [the longest x2 287 us: shards(): left_factor = lax.psum(left_term, ('dp', 'pair')) / group_size]
    pallas_call x0 -> x1, Pallas kernels: none -> 118 us  [shards(): pl.pallas_call(kernel, out_shape=(jax.ShapeDtypeStruct((OUT_L, RANK), F32...]
    dot_general x7 -> x0, matrix products: 107 us -> none  [the longest x2 58.3 us: times_factor(): return jnp.dot(merged_block, factor, precision=lax.Precision.HIGHEST)]
    another operation x15 -> x0, other arithmetic: 20.1 us -> none  [the longest x9 10.8 us: orthonormal(): lower_factor = jnp.linalg.cholesky(gram_total)]
  transfers between devices with their start and end apart: 4 -> 0, of which waited for: 4 -> 0; matrix products, arithmetic and copies ran while one was open for 0% -> 0% of each run, Pallas kernels for 0% -> 0%
where the time goes in v1:
time: 124 us
  Pallas kernels  118 us (95%)
  local copies, waits for them, and re-layouts  5.62 us (5%)
    pallas_call x1, Pallas kernels, shards(): pl.pallas_call(kernel, out_shape=(jax.ShapeDtypeStruct((OUT_L, RANK), F32...  118 us
    unnamed x3, local copies, waits for them, and re-layouts  5.62 us

profile of v1, /device:TPU:1, one launch (start us, length us, event | category | flops | bytes accessed | tf_op | source)
XLA Modules:
  0.0 123.8 jit_solution(11056448953809400708)
XLA Ops:
  0.6 3.0 %copy.5.start = f32[4096,32]{1,0:T(8,128)} copy(f32[4096,32]{0,1:T(8,128)} %param.5) | data formatting | bytes 1048576 | tf_op args[2]
  3.6 117.5 %shard_map.50 = (f32[12,32]{1,0:T(8,128)}, f32[32,32]{1,0:T(8,128)}) custom-call(bf16[1,1536,4096]{2,1,0:T(8,128)(2,1)} %grads.1, bf16[1,1536,4096]{2,1,0:T(8,128)(2,1)} %errors.1, f32[4096,32]{1,0:T(8,128)} %copy.5.start), custom_call_target="tpu_custom_call" | custom-call | tf_op jit(solution)/shard_map/pallas_call | solution.py:323
  121.2 1.3 %copy.8 = f32[12,32]{1,0:T(8,128)} copy(f32[12,32]{1,0:T(8,128)} %get-tuple-element.4) | data formatting | bytes 3072
  122.5 1.3 %copy.9 = f32[32,32]{1,0:T(8,128)} copy(f32[32,32]{1,0:T(8,128)} %get-tuple-element.5) | data formatting | bytes 8192

commit v2 on v1

--- a/solution.py
+++ b/solution.py
@@ -17,9 +17,15 @@
 GROUPS = RANK // 8
 TL = D // 128 * GROUPS
 ROWS = 256
-COLS = 512
+ROWS2 = 512
+COLS = 1024
+ROWS2 = 512
+STEPS_X = FF // COLS
+CHIPS = N // CORES
+PLANE = CHIPS // X
 SCALE = 1.0 / N
 OUT_L, OUT_R = D // N, FF // N
+OUT_AT = -(-OUT_L // 8) * 8
 
 NT = (((1,), (1,)), ((), ()))
 
@@ -36,18 +42,48 @@
     return (t * N) // TL
 
 
-def far_first(k):
+def hops(step):
+    return sum(min(s, n - s) for s, n in zip(step, (X, Y, PAIR)))
+
+
+STEPS = sorted(
+    ((x, y, z, c) for x in range(X) for y in range(Y) for z in range(PAIR) for c in range(CORES) if x or y or z or c),
+    key=lambda step: (-hops(step), (step[0] + 2 * step[1] + 3 * step[2]) % 4, step),
+)
+
+
+def peers():
     dp, z = lax.axis_index("dp"), lax.axis_index("pair")
     x, y, c = dp // (Y * CORES), (dp // CORES) % Y, dp % CORES
-
-    def step(t):
-        return ((3 - t) * (4 - t) // 2) % 4
-
-    x = (x + step(k // 32)) % X
-    y = (y + step((k // 8) % 4)) % Y
-    z = (z + step((k // 2) % 4)) % PAIR
-    c = (c + 1 - k % 2) % CORES
-    return ((x * Y + y) * CORES + c, z)
+    xs = [((x + i) % X) * (Y * CORES) for i in range(X)]
+    ys = [((y + i) % Y) * CORES for i in range(Y)]
+    zs = [(z + i) % PAIR for i in range(PAIR)]
+    cs = [(c + i) % CORES for i in range(CORES)]
+    xy = [[i + j for j in ys] for i in xs]
+    return [(xy[i][j] + cs[m], zs[k]) for i, j, k, m in STEPS]
+
+
+def nearest(i):
+    return (i * (i + 1) // 2) % X
+
+
+def place():
+    dp, z = lax.axis_index("dp"), lax.axis_index("pair")
+    return dp // (Y * CORES), (dp // CORES) % Y, z, dp % CORES
+
+
+def chip_device(chip, core):
+    return ((chip // PAIR) * CORES + core, chip % PAIR)
+
+
+def same_core_peers(i):
+    x, y, z, c = place()
+    base = ((x + X - nearest(i)) % X) * (Y * CORES) + c
+    out = []
+    for k, j in ((k, j) for k in (2, 1, 3, 0) for j in (2, 1, 3, 0)):
+        if i or k or j:
+            out.append((base + ((y + j) % Y) * CORES, (z + k) % PAIR))
+    return out
 
 
 def split(x):
@@ -97,7 +133,7 @@
 
 
 def total(ref):
-    sums = [jnp.sum(ref[i * 16:(i + 1) * 16], axis=0) for i in range(N // 16)]
+    sums = [jnp.sum(ref[i * 16:(i + 1) * 16], axis=0) for i in range(ref.shape[0] // 16)]
     while len(sums) > 1:
         sums = [a + b for a, b in zip(sums[::2], sums[1::2])]
     return sums[0] * SCALE
@@ -108,10 +144,14 @@
 
 
 def kernel(
-    grads, errors, start, left_out, right_out,
-    g, e, q, b_parts, l_parts, l_send, l_recv, l_all, r_send, r_recv, r_all, tile, left, load_sem, send_sem, recv_sem,
+    grads, errors, start, out,
+    g, e, q, b_parts, l_parts, l_send, l_recv, l_all, r_send, r_pair, r_half, r_recv, r_all, tile, left,
+    load_sem, send_sem, recv_sem, pair_send, pair_recv,
 ):
     me = position()
+    my_x, my_y, my_z, core = place()
+    my_chip = (my_x * Y + my_y) * PAIR + my_z
+    partner = chip_device(my_chip, 1 - core)
     my_left = (me * TL + N - 1) // N
     owns_left = jnp.logical_and(my_left < TL, owner_of_left(my_left) == me)
     chunks = D // ROWS
@@ -145,7 +185,7 @@
 
     def turn(j, carry):
         rows = pl.ds(pl.multiple_of(j * 128, 128), 128)
-        put_parts(b_parts, rows, q[rows, :].T)
+        put_parts(b_parts, rows, q[:, rows])
         return carry
 
     lax.fori_loop(0, FF // 128, turn, 0)
@@ -164,56 +204,80 @@
         def _():
             l_recv[it, me] = l_send[it, t]
 
-    def left_chunk(it, i):
+    def send_left(it, chunk, size, acc):
+        tiles = size // 128 * GROUPS
+        for j in range(tiles):
+            lanes = slice(j // GROUPS * 128, j // GROUPS * 128 + 128)
+            ranks = slice(j % GROUPS * 8, j % GROUPS * 8 + 8)
+            l_send[it, chunk * tiles + j] = acc[ranks, lanes]
+
+        def send(j, carry):
+            to_left_owner(it, chunk * tiles + j)
+            return carry
+
+        lax.fori_loop(0, tiles, send, 0)
+
+    def left_chunk(i):
         chunk = (first_chunk + i) % chunks
         rows = pl.ds(pl.multiple_of(chunk * ROWS, ROWS), ROWS)
         parts = b_parts[0:PARTS * RANK, :]
         acc = lax.dot_general(parts, g[rows, :], NT, preferred_element_type=F32)
         acc = acc + lax.dot_general(parts, e[rows, :], NT, preferred_element_type=F32)
-        acc = add_parts(acc)
-        tiles = ROWS // 128 * GROUPS
-        for j in range(tiles):
-            lanes = slice(j // GROUPS * 128, j // GROUPS * 128 + 128)
-            ranks = slice(j % GROUPS * 8, j % GROUPS * 8 + 8)
-            l_send[it, chunk * tiles + j] = acc[ranks, lanes]
-
-        def send(j, carry):
-            to_left_owner(it, chunk * tiles + j)
-            return carry
-
-        lax.fori_loop(0, tiles, send, 0)
+        send_left(0, chunk, ROWS, add_parts(acc))
 
     def right_chunk(it, i):
-        steps = FF // COLS
-        chunk = ((me * steps) // N + steps // 2 + i) % steps
-        columns = pl.ds(pl.multiple_of(chunk * COLS, COLS), COLS)
+        x = (my_x + nearest(STEPS_X - 1 - i)) % X
+        columns = pl.ds(pl.multiple_of(x * COLS, COLS), COLS)
         parts = l_parts[0:PARTS * RANK, :]
         acc = jnp.dot(parts, g[:, columns], preferred_element_type=F32)
         acc = acc + jnp.dot(parts, e[:, columns], preferred_element_type=F32)
         acc = add_parts(acc)
-        owners = COLS // OUT_R
         for j in range(COLS // 128):
             tiles = [acc[r * 8:r * 8 + 8, j * 128:j * 128 + 128] for r in range(GROUPS)]
-            for r in range(128 // OUT_R):
-                r_send[it, chunk * owners + j * (128 // OUT_R) + r] = regroup(tiles, r)
+            for r in range(PAIR):
+                r_send[it, j % CORES, x * PLANE + j // CORES * PAIR + r] = regroup(tiles, r)
+        chips = pl.ds(x * PLANE, PLANE)
+        pltpu.make_async_remote_copy(
+            r_send.at[it, 1 - core, chips], r_pair.at[it, chips], pair_send.at[it], pair_recv.at[it, i],
+            device_id=partner, device_id_type=MESH,
+        ).start()
+
+    def right_pair(it, i):
+        x = (my_x + nearest(STEPS_X - 1 - i)) % X
+        chips = pl.ds(x * PLANE, PLANE)
+        wait_tiles(r_pair.at[it, chips], PLANE, pair_recv.at[it, i])
+        r_half[it, chips] = r_send[it, core, chips] + r_pair[it, chips]
 
         def send(j, carry):
-            owner = chunk * owners + j
-
-            @pl.when(owner != me)
+            chip = x * PLANE + j
+
+            @pl.when(chip != my_chip)
             def _():
                 pltpu.make_async_remote_copy(
-                    r_send.at[it, owner], r_recv.at[it, me], send_sem.at[2 * it + 1], recv_sem.at[2 * it + 1],
-                    device_id=device(owner), device_id_type=MESH,
+                    r_half.at[it, chip], r_recv.at[it, my_chip], send_sem.at[2 * it + 1], recv_sem.at[2 * it + 1],
+                    device_id=chip_device(chip, core), device_id_type=MESH,
                 ).start()
 
-            @pl.when(owner == me)
+            @pl.when(chip == my_chip)
             def _():
-                r_recv[it, me] = r_send[it, owner]
+                r_recv[it, my_chip] = r_half[it, chip]
 
             return carry
 
-        lax.fori_loop(0, owners, send, 0)
+        lax.fori_loop(0, PLANE, send, 0)
+
+    def right_product(it):
+        def step(i, carry):
+            right_chunk(it, i)
+
+            @pl.when(i > 0)
+            def _():
+                right_pair(it, i - 1)
+
+            return carry
+
+        lax.fori_loop(0, STEPS_X, step, 0)
+        right_pair(it, STEPS_X - 1)
 
     def send_left_sums(it):
         @pl.when(owns_left)
@@ -221,14 +285,11 @@
             wait_tiles(l_recv.at[it], N - 1, recv_sem.at[2 * it])
             tile[it] = total(l_recv.at[it])
 
-            def send(k, carry):
+            for peer in peers():
                 pltpu.make_async_remote_copy(
                     tile.at[it], l_all.at[it, my_left], send_sem.at[4 + it], recv_sem.at[4 + it],
-                    device_id=far_first(k), device_id_type=MESH,
+                    device_id=peer, device_id_type=MESH,
                 ).start()
-                return carry
-
-            lax.fori_loop(0, N - 1, send, 0)
             l_all[it, my_left] = tile[it]
             wait_tiles(l_all.at[it], TL - 1, recv_sem.at[4 + it])
 
@@ -237,7 +298,7 @@
             wait_tiles(l_all.at[it], TL, recv_sem.at[4 + it])
 
     def right_sum(it, inverse):
-        wait_tiles(r_recv.at[it], N - 1, recv_sem.at[2 * it + 1])
+        wait_tiles(r_recv.at[it], CHIPS - 1, recv_sem.at[2 * it + 1])
         summed = total(r_recv.at[it])
         ranks = [pltpu.roll(summed, (128 - RANK * r) % 128, 1) if r else summed for r in range(GROUPS)]
         return jnp.dot(inverse, jnp.concatenate(ranks, axis=0), precision=EXACT, preferred_element_type=F32)
@@ -247,12 +308,12 @@
             copy.wait()
         if i == 0:
             pl.semaphore_wait(barrier, N - 1)
-        left_chunk(0, i)
+        left_chunk(i)
     send_left_sums(0)
     for j in range(D // 128):
         block = jnp.concatenate([l_all[0, j * GROUPS + r] for r in range(GROUPS)], axis=0)
         put_parts(l_parts, slice(j * 128, j * 128 + 128), block)
-    lax.fori_loop(0, FF // COLS, lambda i, carry: (right_chunk(0, i), carry)[1], 0)
+    right_product(0)
     inverse = inverse_factor(l_parts)
     mine = right_sum(0, inverse)
     packed = mine[0:8]
@@ -261,26 +322,68 @@
         packed = jnp.where(group == r, pltpu.roll(mine[r * 8:r * 8 + 8], RANK * r, 1), packed)
     tile[2] = packed
 
-    def send_right(k, carry):
+    r_all[core, my_chip] = tile[2]
+
+    def send_right(i):
+        for peer in same_core_peers(i):
+            pltpu.make_async_remote_copy(
+                tile.at[2], r_all.at[core, my_chip], send_sem.at[6], recv_sem.at[6 + my_x],
+                device_id=peer, device_id_type=MESH,
+            ).start()
+
+    def plane(i):
+        return (my_x + nearest(i)) % X
+
+    def pass_on(i):
+        chips = pl.ds(plane(i) * PLANE, PLANE)
+        tiles = r_all.at[core, chips]
+        wait_tiles(tiles, PLANE - 1 if i == 0 else PLANE, recv_sem.at[6 + plane(i)])
         pltpu.make_async_remote_copy(
-            tile.at[2], r_all.at[me], send_sem.at[6], recv_sem.at[6],
-            device_id=far_first(k), device_id_type=MESH,
+            tiles, tiles, pair_send.at[2], pair_recv.at[2, i], device_id=partner, device_id_type=MESH
         ).start()
+
+    def unpack(i):
+        chips = pl.ds(plane(i) * PLANE, PLANE)
+        wait_tiles(r_all.at[1 - core, chips], PLANE, pair_recv.at[2, i])
+        for j in range(COLS // 128):
+            four = [r_all[j % CORES, plane(i) * PLANE + j // CORES * PAIR + r] for r in range(PAIR)]
+            block = jnp.concatenate([regroup(four, r) for r in range(GROUPS)], axis=0)
+            put_parts(b_parts, slice(i * COLS + j * 128, i * COLS + j * 128 + 128), block)
+
+    def some_columns(i, rows):
+        columns = pl.ds(pl.multiple_of(plane(i) * COLS, COLS), COLS)
+        parts = b_parts[0:PARTS * RANK, i * COLS:i * COLS + COLS]
+        acc = lax.dot_general(parts, g[rows, columns], NT, preferred_element_type=F32)
+        acc = acc + lax.dot_general(parts, e[rows, columns], NT, preferred_element_type=F32)
+        return add_parts(acc)
+
+    def columns_step(i, r):
+        rows = slice(r, r + ROWS2)
+        if i == 0:
+            left[:, rows] = some_columns(i, rows)
+        else:
+            left[:, rows] += some_columns(i, rows)
+
+    for i in range(STEPS_X - 1):
+        send_right(i)
+    pass_on(0)
+    send_right(STEPS_X - 1)
+    unpack(0)
+    for i in range(STEPS_X - 1):
+        pass_on(i + 1)
+        columns_step(i, 0)
+        unpack(i + 1)
+        for r in range(ROWS2, D, ROWS2):
+            columns_step(i, r)
+
+    def last_columns(i, carry):
+        steps = D // ROWS2
+        chunk = ((me * steps) // N + steps // 2 + i) % steps
+        rows = pl.ds(pl.multiple_of(chunk * ROWS2, ROWS2), ROWS2)
+        send_left(1, chunk, ROWS2, left[:, rows] + some_columns(STEPS_X - 1, rows))
         return carry
 
-    lax.fori_loop(0, N - 1, send_right, 0)
-    r_all[me] = tile[2]
-    wait_tiles(r_all, N - 1, recv_sem.at[6])
-
-    def gather_right(j, carry):
-        tiles = [r_all[j * 4 + r] for r in range(4)]
-        block = jnp.concatenate([regroup(tiles, r) for r in range(GROUPS)], axis=0)
-        put_parts(b_parts, pl.ds(pl.multiple_of(j * 128, 128), 128), block)
-        return carry
-
-    lax.fori_loop(0, FF // 128, gather_right, 0)
-
-    lax.fori_loop(0, chunks, lambda i, carry: (left_chunk(1, i), carry)[1], 0)
+    lax.fori_loop(0, D // ROWS2, last_columns, 0)
     inverse = inverse_factor(b_parts)
     send_left_sums(1)
     for j in range(D // 512):
@@ -294,62 +397,66 @@
         block = jnp.dot(inverse, block, precision=EXACT, preferred_element_type=F32)
         left[:, j * 512:j * 512 + 512] = block
         put_parts(l_parts, slice(j * 512, j * 512 + 512), block)
-    lax.fori_loop(0, FF // COLS, lambda i, carry: (right_chunk(1, i), carry)[1], 0)
+    right_product(1)
     at = (me * OUT_L) // 128
     block = left[:, pl.ds(pl.multiple_of(at * 128, 128), 256)]
     block = pltpu.roll(block, (256 - (me * OUT_L - at * 128)) % 256, 1)[:, 0:128]
-    left_out[...] = block.T[0:OUT_L, :]
+    out[0:OUT_L, :] = block.T[0:OUT_L, :]
     inverse = inverse_factor(l_parts)
     mine = right_sum(1, inverse)
-    right_out[...] = mine.T[0:OUT_R, :]
+    out[OUT_AT:OUT_AT + OUT_R, :] = mine.T[0:OUT_R, :]
 
     for it in range(2):
         @pl.when(owns_left)
         def _():
             wait_tiles(l_send.at[it], TL - 1, send_sem.at[2 * it])
-            wait_tiles(r_send.at[it], N - 1, send_sem.at[4 + it])
+            wait_tiles(l_recv.at[it], N - 1, send_sem.at[4 + it])
 
         @pl.when(jnp.logical_not(owns_left))
         def _():
             wait_tiles(l_send.at[it], TL, send_sem.at[2 * it])
 
-        wait_tiles(r_send.at[it], N - 1, send_sem.at[2 * it + 1])
-    wait_tiles(r_all, N - 1, send_sem.at[6])
+        wait_tiles(r_half.at[it], CHIPS - 1, send_sem.at[2 * it + 1])
+        wait_tiles(r_pair.at[it], CHIPS, pair_send.at[it])
+    wait_tiles(r_all.at[0], CHIPS - 1, send_sem.at[6])
+    wait_tiles(r_all.at[0], CHIPS, pair_send.at[2])
 
 
 def shards(local_grads, error_feedback, q_start):
     anywhere = pl.BlockSpec(memory_space=pl.ANY)
     vmem = pl.BlockSpec(memory_space=pltpu.VMEM)
-    return pl.pallas_call(
+    out = pl.pallas_call(
         kernel,
-        out_shape=(
-            jax.ShapeDtypeStruct((OUT_L, RANK), F32),
-            jax.ShapeDtypeStruct((OUT_R, RANK), F32),
-        ),
+        out_shape=jax.ShapeDtypeStruct((OUT_AT + OUT_R, RANK), F32),
         in_specs=[anywhere, anywhere, anywhere],
-        out_specs=(vmem, vmem),
+        out_specs=vmem,
         scratch_shapes=[
             pltpu.VMEM((D, FF), BF16),
             pltpu.VMEM((D, FF), BF16),
-            pltpu.VMEM((FF, RANK), F32),
+            pltpu.VMEM((RANK, FF), F32),
             pltpu.VMEM((128, FF), BF16),
             pltpu.VMEM((128, D), BF16),
             pltpu.VMEM((2, TL, 8, 128), F32),
             pltpu.VMEM((2, N, 8, 128), F32),
             pltpu.VMEM((2, TL, 8, 128), F32),
-            pltpu.VMEM((2, N, 8, 128), F32),
-            pltpu.VMEM((2, N, 8, 128), F32),
-            pltpu.VMEM((N, 8, 128), F32),
+            pltpu.VMEM((2, CORES, CHIPS, 8, 128), F32),
+            pltpu.VMEM((2, CHIPS, 8, 128), F32),
+            pltpu.VMEM((2, CHIPS, 8, 128), F32),
+            pltpu.VMEM((2, CHIPS, 8, 128), F32),
+            pltpu.VMEM((CORES, CHIPS, 8, 128), F32),
             pltpu.VMEM((3, 8, 128), F32),
             pltpu.VMEM((RANK, D + 128), F32),
             pltpu.SemaphoreType.DMA((2 * (D // ROWS) + 1,)),
             pltpu.SemaphoreType.DMA((7,)),
-            pltpu.SemaphoreType.DMA((7,)),
+            pltpu.SemaphoreType.DMA((6 + X,)),
+            pltpu.SemaphoreType.DMA((3,)),
+            pltpu.SemaphoreType.DMA((3, STEPS_X)),
         ],
         compiler_params=pltpu.CompilerParams(
             vmem_limit_bytes=60 << 20, collective_id=0, has_side_effects=True
         ),
-    )(local_grads, error_feedback, q_start)
+    )(local_grads, error_feedback, q_start.T)
+    return (out[0:OUT_L], out[OUT_AT:OUT_AT + OUT_R])
 
 
 def solution(mesh):

time: 124 us -> 97 us (0.78)
  Pallas kernels: 118 us -> 93.5 us
  local copies, waits for them, and re-layouts: 5.62 us -> 2.62 us
    pallas_call x1, Pallas kernels: 118 us -> 93.5 us  [shards(): pl.pallas_call(kernel, out_shape=jax.ShapeDtypeStruct((OUT_AT + OUT_R, RA...]
    unnamed x3 -> x0, local copies, waits for them, and re-layouts: 5.62 us -> none
    slice x0 -> x2, local copies, waits for them, and re-layouts: none -> 2.62 us  [shards(): return (out[0:OUT_L], out[OUT_AT:OUT_AT + OUT_R])]
where the time goes in v2:
time: 97 us; the launch traced here: 96.8 us
  Pallas kernels  93.5 us (96%)
  local copies, waits for them, and re-layouts  2.62 us (3%)
    pallas_call x1, Pallas kernels, shards(): pl.pallas_call(kernel, out_shape=jax.ShapeDtypeStruct((OUT_AT + OUT_R, RA...  93.5 us
    slice x2, local copies, waits for them, and re-layouts, shards(): return (out[0:OUT_L], out[OUT_AT:OUT_AT + OUT_R])  2.62 us

profile of v2, /device:TPU:1, one launch (start us, length us, event | category | flops | bytes accessed | tf_op | source)
XLA Modules:
  0.0 96.8 jit_solution(11941798304111169966)
XLA Ops:
  0.6 93.5 %shard_map.50 = f32[48,32]{1,0:T(8,128)} custom-call(bf16[1,1536,4096]{2,1,0:T(8,128)(2,1)} %grads.1, bf16[1,1536,4096]{2,1,0:T(8,128)(2,1)} %errors.1, f32[32,4096]{1,0:T(8,128)} %bitcast.1), custom_call_target="tpu_custom_call" | custom-call | tf_op jit(solution)/shard_map/pallas_call | solution.py:428
  94.2 1.3 %slice.6 = f32[12,32]{1,0:T(8,128)} slice(f32[48,32]{1,0:T(8,128)} %shard_map.50), slice={[0:12], [0:32]} | slice | bytes 3072 | tf_op jit(solution)/shard_map/slice | solution.py:459
  95.5 1.3 %slice.7 = f32[32,32]{1,0:T(8,128)} slice(f32[48,32]{1,0:T(8,128)} %shard_map.50), slice={[16:48], [0:32]} | slice | bytes 8192 | tf_op jit(solution)/shard_map/slice | solution.py:459

commit v3 on v2

--- a/solution.py
+++ b/solution.py
@@ -1,3 +1,5 @@
+import functools
+
 import jax
 import jax.numpy as jnp
 from jax import lax
@@ -16,8 +18,7 @@
 PARTS = 3
 GROUPS = RANK // 8
 TL = D // 128 * GROUPS
-ROWS = 256
-ROWS2 = 512
+ROWS = 512
 COLS = 1024
 ROWS2 = 512
 STEPS_X = FF // COLS
@@ -204,18 +205,18 @@
         def _():
             l_recv[it, me] = l_send[it, t]
 
-    def send_left(it, chunk, size, acc):
+    def put_left(it, chunk, size, acc):
         tiles = size // 128 * GROUPS
         for j in range(tiles):
             lanes = slice(j // GROUPS * 128, j // GROUPS * 128 + 128)
             ranks = slice(j % GROUPS * 8, j % GROUPS * 8 + 8)
             l_send[it, chunk * tiles + j] = acc[ranks, lanes]
 
-        def send(j, carry):
+    def send_left(it, chunk, size):
+        tiles = size // 128 * GROUPS
+
+        for j in range(tiles):
             to_left_owner(it, chunk * tiles + j)
-            return carry
-
-        lax.fori_loop(0, tiles, send, 0)
 
     def left_chunk(i):
         chunk = (first_chunk + i) % chunks
@@ -223,7 +224,7 @@
         parts = b_parts[0:PARTS * RANK, :]
         acc = lax.dot_general(parts, g[rows, :], NT, preferred_element_type=F32)
         acc = acc + lax.dot_general(parts, e[rows, :], NT, preferred_element_type=F32)
-        send_left(0, chunk, ROWS, add_parts(acc))
+        put_left(0, chunk, ROWS, add_parts(acc))
 
     def right_chunk(it, i):
         x = (my_x + nearest(STEPS_X - 1 - i)) % X
@@ -242,29 +243,28 @@
             device_id=partner, device_id_type=MESH,
         ).start()
 
-    def right_pair(it, i):
+    def right_pair(it, i, own):
         x = (my_x + nearest(STEPS_X - 1 - i)) % X
         chips = pl.ds(x * PLANE, PLANE)
         wait_tiles(r_pair.at[it, chips], PLANE, pair_recv.at[it, i])
         r_half[it, chips] = r_send[it, core, chips] + r_pair[it, chips]
 
-        def send(j, carry):
+        def send(chip):
+            pltpu.make_async_remote_copy(
+                r_half.at[it, chip], r_recv.at[it, my_chip], send_sem.at[2 * it + 1], recv_sem.at[2 * it + 1],
+                device_id=chip_device(chip, core), device_id_type=MESH,
+            ).start()
+
+        for j in range(PLANE):
             chip = x * PLANE + j
-
-            @pl.when(chip != my_chip)
-            def _():
-                pltpu.make_async_remote_copy(
-                    r_half.at[it, chip], r_recv.at[it, my_chip], send_sem.at[2 * it + 1], recv_sem.at[2 * it + 1],
-                    device_id=chip_device(chip, core), device_id_type=MESH,
-                ).start()
-
-            @pl.when(chip == my_chip)
-            def _():
-                r_recv[it, my_chip] = r_half[it, chip]
-
-            return carry
-
-        lax.fori_loop(0, PLANE, send, 0)
+            if not own:
+                send(chip)
+                continue
+
+            pl.when(chip != my_chip)(functools.partial(send, chip))
+
+        if own:
+            r_recv[it, my_chip] = r_half[it, my_chip]
 
     def right_product(it):
         def step(i, carry):
@@ -272,12 +272,12 @@
 
             @pl.when(i > 0)
             def _():
-                right_pair(it, i - 1)
+                right_pair(it, i - 1, False)
 
             return carry
 
         lax.fori_loop(0, STEPS_X, step, 0)
-        right_pair(it, STEPS_X - 1)
+        right_pair(it, STEPS_X - 1, True)
 
     def send_left_sums(it):
         @pl.when(owns_left)
@@ -306,9 +306,12 @@
     for i in range(chunks):
         for copy in load(i):
             copy.wait()
-        if i == 0:
+        left_chunk(i)
+        if i == 1:
             pl.semaphore_wait(barrier, N - 1)
-        left_chunk(i)
+            send_left(0, first_chunk % chunks, ROWS)
+        if i >= 1:
+            send_left(0, (first_chunk + i) % chunks, ROWS)
     send_left_sums(0)
     for j in range(D // 128):
         block = jnp.concatenate([l_all[0, j * GROUPS + r] for r in range(GROUPS)], axis=0)
@@ -380,7 +383,8 @@
         steps = D // ROWS2
         chunk = ((me * steps) // N + steps // 2 + i) % steps
         rows = pl.ds(pl.multiple_of(chunk * ROWS2, ROWS2), ROWS2)
-        send_left(1, chunk, ROWS2, left[:, rows] + some_columns(STEPS_X - 1, rows))
+        put_left(1, chunk, ROWS2, left[:, rows] + some_columns(STEPS_X - 1, rows))
+        send_left(1, chunk, ROWS2)
         return carry
 
     lax.fori_loop(0, D // ROWS2, last_columns, 0)
@@ -420,6 +424,11 @@
         wait_tiles(r_pair.at[it], CHIPS, pair_send.at[it])
     wait_tiles(r_all.at[0], CHIPS - 1, send_sem.at[6])
     wait_tiles(r_all.at[0], CHIPS, pair_send.at[2])
+
+
+def hand_out(both, left, right):
+    left[...] = both[0:OUT_L, :]
+    right[...] = both[OUT_AT:OUT_AT + OUT_R, :]
 
 
 def shards(local_grads, error_feedback, q_start):
@@ -456,7 +465,13 @@
             vmem_limit_bytes=60 << 20, collective_id=0, has_side_effects=True
         ),
     )(local_grads, error_feedback, q_start.T)
-    return (out[0:OUT_L], out[OUT_AT:OUT_AT + OUT_R])
+    return pl.pallas_call(
+        hand_out,
+        out_shape=(
+            jax.ShapeDtypeStruct((OUT_L, RANK), F32),
+            jax.ShapeDtypeStruct((OUT_R, RANK), F32),
+        ),
+    )(out)
 
 
 def solution(mesh):

time: 97 us -> 85.1 us (0.88)
  Pallas kernels: 93.5 us -> 84.2 us
  local copies, waits for them, and re-layouts: 2.62 us -> 0 us
    pallas_call x1, Pallas kernels: 93.5 us -> 82.9 us  [shards(): pl.pallas_call(kernel, out_shape=jax.ShapeDtypeStruct((OUT_AT + OUT_R, RA...]
    slice x2 -> x0, local copies, waits for them, and re-layouts: 2.62 us -> none  [shards(): return (out[0:OUT_L], out[OUT_AT:OUT_AT + OUT_R])]
    pallas_call x0 -> x1, Pallas kernels: none -> 1.35 us  [shards(): pl.pallas_call(hand_out, out_shape=(jax.ShapeDtypeStruct((OUT_L, RANK), F...]
where the time goes in v3:
time: 85.1 us; the launch traced here: 84.9 us
  Pallas kernels  84.2 us (99%)
    pallas_call x1, Pallas kernels, shards(): pl.pallas_call(kernel, out_shape=jax.ShapeDtypeStruct((OUT_AT + OUT_R, RA...  82.9 us

profile of v3, /device:TPU:1, one launch (start us, length us, event | category | flops | bytes accessed | tf_op | source)
XLA Modules:
  0.0 84.9 jit_solution(18284688440930368648)
XLA Ops:
  0.6 82.9 %shard_map.50.both = f32[48,32]{1,0:T(8,128)} custom-call(bf16[1,1536,4096]{2,1,0:T(8,128)(2,1)} %grads.1, bf16[1,1536,4096]{2,1,0:T(8,128)(2,1)} %errors.1, f32[32,4096]{1,0:T(8,128)} %bitcast.1), custom_call_target="tpu_custom_call" | custom-call | tf_op jit(solution)/shard_map/pallas_call | solution.py:437
  83.5 1.4 %shard_map.51 = (f32[12,32]{1,0:T(8,128)}, f32[32,32]{1,0:T(8,128)}) custom-call(f32[48,32]{1,0:T(8,128)} %shard_map.50.both), custom_call_target="tpu_custom_call" | custom-call | tf_op jit(solution)/shard_map/pallas_call | solution.py:468

commit v4 on v3

--- a/solution.py
+++ b/solution.py
@@ -147,7 +147,7 @@
 def kernel(
     grads, errors, start, out,
     g, e, q, b_parts, l_parts, l_send, l_recv, l_all, r_send, r_pair, r_half, r_recv, r_all, tile, left,
-    load_sem, send_sem, recv_sem, pair_send, pair_recv,
+    load_sem, send_sem, far_send, recv_sem, pair_send, pair_recv,
 ):
     me = position()
     my_x, my_y, my_z, core = place()
@@ -330,7 +330,7 @@
     def send_right(i):
         for peer in same_core_peers(i):
             pltpu.make_async_remote_copy(
-                tile.at[2], r_all.at[core, my_chip], send_sem.at[6], recv_sem.at[6 + my_x],
+                tile.at[2], r_all.at[core, my_chip], send_sem.at[6] if i < 2 else far_send, recv_sem.at[6 + my_x],
                 device_id=peer, device_id_type=MESH,
             ).start()
 
@@ -367,10 +367,11 @@
         else:
             left[:, rows] += some_columns(i, rows)
 
-    for i in range(STEPS_X - 1):
+    for i in range(STEPS_X):
+        if i == 2:
+            wait_tiles(r_all.at[0], 2 * PLANE - 1, send_sem.at[6])
         send_right(i)
     pass_on(0)
-    send_right(STEPS_X - 1)
     unpack(0)
     for i in range(STEPS_X - 1):
         pass_on(i + 1)
@@ -422,7 +423,7 @@
 
         wait_tiles(r_half.at[it], CHIPS - 1, send_sem.at[2 * it + 1])
         wait_tiles(r_pair.at[it], CHIPS, pair_send.at[it])
-    wait_tiles(r_all.at[0], CHIPS - 1, send_sem.at[6])
+    wait_tiles(r_all.at[0], 2 * PLANE, far_send)
     wait_tiles(r_all.at[0], CHIPS, pair_send.at[2])
 
 
@@ -457,6 +458,7 @@
             pltpu.VMEM((RANK, D + 128), F32),
             pltpu.SemaphoreType.DMA((2 * (D // ROWS) + 1,)),
             pltpu.SemaphoreType.DMA((7,)),
+            pltpu.SemaphoreType.DMA(()),
             pltpu.SemaphoreType.DMA((6 + X,)),
             pltpu.SemaphoreType.DMA((3,)),
             pltpu.SemaphoreType.DMA((3, STEPS_X)),

time: 85.1 us -> 84.8 us (level)
  no operation moved by 1% of the time
where the time goes in v4:
time: 84.8 us; the launch traced here: 84.6 us
  Pallas kernels  84 us (99%)
    pallas_call x1, Pallas kernels, shards(): pl.pallas_call(kernel, out_shape=jax.ShapeDtypeStruct((OUT_AT + OUT_R, RA...  82.6 us

profile of v4, /device:TPU:1, one launch (start us, length us, event | category | flops | bytes accessed | tf_op | source)
XLA Modules:
  0.0 84.6 jit_solution(7212977539228860065)
XLA Ops:
  0.6 82.6 %shard_map.50.both = f32[48,32]{1,0:T(8,128)} custom-call(bf16[1,1536,4096]{2,1,0:T(8,128)(2,1)} %grads.1, bf16[1,1536,4096]{2,1,0:T(8,128)(2,1)} %errors.1, f32[32,4096]{1,0:T(8,128)} %bitcast.1), custom_call_target="tpu_custom_call" | custom-call | tf_op jit(solution)/shard_map/pallas_call | solution.py:438
  83.2 1.4 %shard_map.51 = (f32[12,32]{1,0:T(8,128)}, f32[32,32]{1,0:T(8,128)}) custom-call(f32[48,32]{1,0:T(8,128)} %shard_map.50.both), custom_call_target="tpu_custom_call" | custom-call | tf_op jit(solution)/shard_map/pallas_call | solution.py:470
